TPU v7x, 128 devices: a whole 4x4x4 slice. The times are simulated.
128 devices in a mesh: req: 64 (over z, y, x), kv: 2 (over core).
Axes of the slice: x: 4, y: 4, z: 4, core: 2. Of those that a mesh axis runs over, the one named last changes fastest.
Arguments:
- queries: bfloat16 [16384, 2048], P(('req', 'kv')), may hold values from -6 to 6
- keys: bfloat16 [16384, 1024], P(('req', 'kv')), may hold values from -6 to 6
- values: bfloat16 [16384, 1024], P(('req', 'kv')), may hold values from -6 to 6
- residual: bfloat16 [16384, 3584], P(('req', 'kv'))
- segment_ids: int32 [16384], P(('req', 'kv')), may hold values from 127 to 16383, as said below
- regroup: int32 [16384], P(('req', 'kv')), may hold values from 0 to 16383, as said below
- out_weight: bfloat16 [2048, 3584], P('kv')
- attn_gain: float32 [3584], replicated, may hold values from 0.1 to 1.9
- pre_gain: float32 [3584], replicated, may hold values from 0.1 to 1.9
- gate_weight: bfloat16 [3584, 7168], P(None, 'kv'), may hold values from -0.09375 to 0.09375
- up_weight: bfloat16 [3584, 7168], P(None, 'kv'), may hold values from -0.09375 to 0.09375
- down_weight: bfloat16 [7168, 3584], P('kv')
- post_gain: float32 [3584], replicated, may hold values from 0.1 to 1.9
Outputs:
- layer_out: bfloat16 [16384, 3584], P(('req', 'kv'))
- key_cache_rows: bfloat16 [4, 16384, 256], P(None, ('req', 'kv'))
- value_cache_rows: bfloat16 [4, 16384, 256], P(None, ('req', 'kv'))
Inputs may be any that keep to these rules, and one draw needn't show every extreme that they name: `segment_ids`: A request is a run of consecutive slots carrying one id, the index of its last slot; no request runs from one index of req's 256 slots into the next. `regroup`: A permutation of the slots. Each device (in req+kv order) sends exactly one of its 128 slots to each of the 128 devices: for every pair of devices, exactly one slot of the first has its output row among the 128 rows of the second.
All inputs are finite; a program needn't handle non-finite values.
Results may differ from a plain program's by a relative error of at most 0.0095.
Values may be sent and summed in bfloat16 or wider, within the bound.
A program may use at most 192 MiB of HBM per device.

v0:
```python
import jax
import jax.numpy as jnp
from jax import lax
from jax.sharding import PartitionSpec as P

QUERY_HEADS = 8
KEY_VALUE_HEADS = 4
HEAD_ENTRIES = 256
WINDOW_REACH = 512
cap_value = 50.0
norm_eps = 1e-06


def from_behind(block, axis, distance):
    devices = range(lax.axis_size(axis))
    route = [(i - distance, i) for i in devices if i - distance in devices]
    return lax.ppermute(block, axis, route)


def rms_scale(values_in, gain_row):
    mean_square = jnp.mean(values_in * values_in, axis=-1, keepdims=True)
    return values_in * lax.rsqrt(mean_square + norm_eps) * gain_row


def key_mask(own_ids, key_ids, key_pos):
    distance = jnp.arange(own_ids.shape[0], dtype=jnp.int32)[:, None] - key_pos[None, :]
    return (own_ids[:, None] == key_ids[None, :]) & (distance >= 0) & (distance < WINDOW_REACH)


def block_terms(query_head_rows, key_heads, value_heads, allowed):
    raw_scores = jnp.einsum(
        "tkgd,skd->kgts", query_head_rows, key_heads, preferred_element_type=jnp.float32
    )
    scores = cap_value * jnp.tanh(raw_scores * HEAD_ENTRIES ** (-0.5) / cap_value)
    weights = jnp.where(allowed, jnp.exp(scores), 0.0)
    totals = jnp.sum(weights, axis=-1)
    numerator = jnp.einsum(
        "kgts,skd->tkgd",
        weights.astype(jnp.bfloat16),
        value_heads,
        preferred_element_type=jnp.float32,
    )
    return (numerator, totals)


def send_rows(normed_part, normed_pos, stream_part, key_portion, value_portion):
    received = (
        lax.all_to_all(normed_part, ("req", "kv"), split_axis=0, concat_axis=0, tiled=True),
        lax.all_to_all(normed_pos, ("req", "kv"), split_axis=0, concat_axis=0, tiled=True),
        lax.all_to_all(stream_part, ("req", "kv"), split_axis=0, concat_axis=0, tiled=True),
        lax.all_to_all(key_portion, ("req", "kv"), split_axis=0, concat_axis=0, tiled=True),
        lax.all_to_all(value_portion, ("req", "kv"), split_axis=0, concat_axis=0, tiled=True),
    )
    return received


def per_device(
    queries,
    keys,
    values,
    residual,
    segment_ids,
    regroup,
    out_weight,
    attn_gain,
    pre_gain,
    gate_weight,
    up_weight,
    down_weight,
    post_gain,
):
    resident_rows = queries.shape[0]
    grouped_heads = QUERY_HEADS // KEY_VALUE_HEADS
    query_head_rows = queries.reshape(resident_rows, KEY_VALUE_HEADS, grouped_heads, HEAD_ENTRIES)
    own_ids = segment_ids + 1
    base_pos = jnp.arange(resident_rows, dtype=jnp.int32)
    key_collections = [(keys, values, own_ids, base_pos)]
    moved_keys, moved_values, moved_ids = from_behind((keys, values, own_ids), "kv", 1)
    key_collections.append((moved_keys, moved_values, moved_ids, base_pos - resident_rows))
    gathered_keys = jnp.concatenate(
        [key_collection[0] for key_collection in key_collections], axis=0
    ).reshape(-1, KEY_VALUE_HEADS, HEAD_ENTRIES)
    gathered_values = jnp.concatenate(
        [key_collection[1] for key_collection in key_collections], axis=0
    ).reshape(-1, KEY_VALUE_HEADS, HEAD_ENTRIES)
    all_ids = jnp.concatenate([key_collection[2] for key_collection in key_collections], axis=0)
    all_pos = jnp.concatenate([key_collection[3] for key_collection in key_collections], axis=0)
    numerator, totals = block_terms(
        query_head_rows, gathered_keys, gathered_values, key_mask(own_ids, all_ids, all_pos)
    )
    attended_output = (
        (numerator / jnp.transpose(totals, (2, 0, 1))[..., None])
        .astype(jnp.bfloat16)
        .reshape(resident_rows, QUERY_HEADS * HEAD_ENTRIES)
    )
    head_rows = lax.all_to_all(attended_output, "kv", split_axis=1, concat_axis=0, tiled=True)
    picked = head_rows
    projected = lax.psum_scatter(
        jnp.dot(picked, out_weight, preferred_element_type=jnp.float32).astype(jnp.bfloat16),
        "kv",
        scatter_dimension=0,
        tiled=True,
    ).astype(jnp.float32)
    stream = (residual.astype(jnp.float32) + rms_scale(projected, attn_gain)).astype(jnp.bfloat16)
    normed = rms_scale(stream.astype(jnp.float32), pre_gain).astype(jnp.bfloat16)
    row_order = jnp.argsort(regroup)
    destination_rows = regroup[row_order]
    sorted_normed = normed[row_order]
    sorted_stream = stream[row_order]
    sorted_keys = keys[row_order]
    sorted_values = values[row_order]
    received = send_rows(
        sorted_normed, destination_rows % resident_rows, sorted_stream, sorted_keys, sorted_values
    )
    placed = jnp.argsort(received[1])
    own_normed = received[0][placed]
    group_normed = lax.all_gather(own_normed, "kv", axis=0, tiled=True)
    own_stream = received[2][placed]
    resident_keys = received[3][placed]
    resident_values = received[4][placed]
    picked = group_normed
    gate_part = jnp.dot(picked, gate_weight, preferred_element_type=jnp.float32)
    up_part = jnp.dot(picked, up_weight, preferred_element_type=jnp.float32)
    active = (jax.nn.gelu(gate_part, approximate=True) * up_part).astype(jnp.bfloat16)
    ffw_sum = lax.psum_scatter(
        jnp.dot(active, down_weight, preferred_element_type=jnp.float32).astype(jnp.bfloat16),
        "kv",
        scatter_dimension=0,
        tiled=True,
    ).astype(jnp.float32)
    layer_out = (own_stream.astype(jnp.float32) + rms_scale(ffw_sum, post_gain)).astype(
        jnp.bfloat16
    )
    key_cache_rows = resident_keys.reshape(resident_rows, KEY_VALUE_HEADS, HEAD_ENTRIES).transpose(
        1, 0, 2
    )
    value_cache_rows = resident_values.reshape(
        resident_rows, KEY_VALUE_HEADS, HEAD_ENTRIES
    ).transpose(1, 0, 2)
    return (layer_out, key_cache_rows, value_cache_rows)


def solution(mesh):
    placed = (
        P(("req", "kv"), None),
        P(("req", "kv"), None),
        P(("req", "kv"), None),
        P(("req", "kv"), None),
        P(("req", "kv")),
        P(("req", "kv")),
        P("kv", None),
        P(),
        P(),
        P(None, "kv"),
        P(None, "kv"),
        P("kv", None),
        P(),
    )
    return jax.shard_map(
        per_device,
        mesh=mesh,
        in_specs=placed,
        out_specs=(
            P(("req", "kv"), None),
            P(None, ("req", "kv"), None),
            P(None, ("req", "kv"), None),
        ),
        check_vma=False,
    )
```

profile of v0, /device:TPU:1, one launch (start us, length us, event | category | flops | bytes accessed | tf_op | source)
XLA Modules:
  0.0 216.2 jit_solution(5172984267959892114)
XLA Ops:
  7.2 0.7 broadcast_add_fusion
  7.9 1.3 collective-permute-start.1
  9.2 1.1 copy.46
  10.3 1.3 collective-permute-start.2
  11.6 1.3 collective-permute-start
  12.9 1.4 reshape.106
  14.4 0.1 fusion.35
  14.5 1.0 collective-permute-done
  15.5 1.0 pad_maximum_fusion
  16.5 0.2 copy.44
  16.8 0.6 fusion.42
  17.4 0.3 fusion.29
  17.7 0.2 copy.50
  17.9 4.2 %all_to_all.76 = bf16[128,2,1024]{2,0,1:T(8,128)(2,1)S(1)} all-to-all(bf16[128,2,1024]{2,0,1:T(8,128)(2,1)S(1)} %copy.50), channel_id=1, replica_groups=mesh['req'=64,'kv'=2] {'kv'}, dimensions={1} | all-to-all | bytes 1048576 | tf_op jit(solution)/shard_map/all_to_all | solution.py:96
  22.1 6.4 %convolution_convert_fusion.1 = bf16[256,3584]{1,0:T(8,128)(2,1)} fusion(bf16[256,1024]{1,0:T(8,128)(2,1)S(1)} %bitcast.76, bf16[1024,3584]{1,0:T(8,128)(2,1)} %param.19), kind=kOutput, calls=%fused_computation.13 | convolution fusion | flops 1879965696 | bytes 9699328 | tf_op jit(solution)/shard_map/dot_general | solution.py:99
  28.6 0.6 copy-done
  29.2 2.5 %sort.31 = (s32[128]{0:T(128)}, s32[128]{0:T(128)S(1)}) sort(s32[128]{0:T(128)S(1)} %copy-done, s32[128]{0:T(128)S(1)} %iota.18), dimensions={0}, to_apply=%region_3.4 | sort | flops 896 | bytes 2048 | tf_op jit(solution)/shard_map/jit(argsort)/sort | solution.py:106
  31.8 1.2 gather_fusion.1
  33.0 0.7 copy.52
  33.8 10.9 %all-to-all-start.2 = ((s32[128,1,1]{2,1,0:T(1,128)}), s32[128,1,1]{2,1,0:T(1,128)S(1)}, u32[]{:S(2)}, u32[]{:S(2)}) async-start(s32[128,1,1]{2,1,0:T(1,128)} %copy.52), calls=%async_computation.3 | async-start | bytes 131072 | tf_op jit(solution)/shard_map/all_to_all | solution.py:49
  44.7 1.4 fusion.8
  46.2 1.8 fusion.12
  48.0 0.3 fusion.14
  48.3 1.1 gather_fusion.3
  49.4 0.5 broadcast.147
  49.9 1.2 reduce.1
  51.1 1.1 reshape.194
  52.2 2.0 all-to-all-done.2
  54.2 7.8 %all-to-all-start.3 = ((bf16[128,2,1792]{2,1,0:T(2,128)(2,1)}), bf16[128,2,1792]{2,1,0:T(2,128)(2,1)S(1)}, u32[]{:S(2)}, u32[]{:S(2)}) async-start(bf16[128,2,1792]{2,1,0:T(2,128)(2,1)} %reshape.194), calls=%async_computation.4 | async-start | bytes 1835008 | tf_op jit(solution)/shard_map/all_to_all | solution.py:48
  62.0 2.4 %reduce = s32[128]{0:T(128)S(1)} reduce(s32[128,1,1]{2,1,0:T(1,128)S(1)} %all-to-all-done.2, s32[]{:T(128)} %constant.17.clone.1), dimensions={1,2}, to_apply=%all_to_all.59.reduce_sub_computation | reduce | bytes 1028 | tf_op jit(solution)/shard_map/all_to_all | solution.py:49
  64.4 2.5 %sort.32 = (s32[128]{0:T(128)}, s32[128]{0:T(128)S(1)}) sort(s32[128]{0:T(128)S(1)} %reduce, s32[128]{0:T(128)S(1)} %iota.19), dimensions={0}, to_apply=%region_4.5 | sort | flops 896 | bytes 2048 | tf_op jit(solution)/shard_map/jit(argsort)/sort | solution.py:115
  67.0 13.0 %all-to-all-done.3 = bf16[128,2,1792]{2,1,0:T(2,128)(2,1)S(1)} async-done(((bf16[128,2,1792]{2,1,0:T(2,128)(2,1)}), bf16[128,2,1792]{2,1,0:T(2,128)(2,1)S(1)}, u32[]{:S(2)}, u32[]{:S(2)}) %all-to-all-start.3) | async-done | bytes 917536 | tf_op jit(solution)/shard_map/all_to_all | solution.py:48
  79.9 2.1 reshape.195
  82.0 1.6 copy.79
  83.7 2.0 gather_fusion.4
  85.7 0.2 reduce-scatter.5.cloned.1.call-start
  86.0 9.3 %all-gather.3.cloned.1.call-done = bf16[256,3584]{1,0:T(8,128)(2,1)} async-done(((bf16[128,3584]{1,0:T(8,128)(2,1)}), bf16[256,3584]{1,0:T(8,128)(2,1)}) %all-gather.3.cloned.1.call-update) | async-done | bytes 1835024 | tf_op jit(solution)/shard_map/all_gather | solution.py:117
  95.3 17.1 %fusion.43 = f32[256,3584]{1,0:T(8,128)} fusion(bf16[256,3584]{1,0:T(8,128)(2,1)} %all-gather.3.cloned.1.call-done, bf16[3584,3584]{1,0:T(8,128)(2,1)} %param.22), kind=kOutput, calls=%fused_computation.86 | convolution fusion | flops 6576668672 | bytes 31195136 | tf_op jit(solution)/shard_map/dot_general | solution.py:122
  112.4 24.6 %convolution_convert_fusion = bf16[256,3584]{1,0:T(8,128)(2,1)} fusion(bf16[3584,3584]{1,0:T(8,128)(2,1)} %param.24, bf16[256,3584]{1,0:T(8,128)(2,1)S(1)} %copy-done.7, bf16[3584,3584]{1,0:T(8,128)(2,1)} %param.23, f32[256,3584]{1,0:T(8,128)} %fusion.43), kind=kOutput, calls=%fused_computation.12 | convolution fusion | flops 13163429888 | bytes 58720256 | tf_op jit(solution)/shard_map/dot_general | solution.py:126
  137.0 0.9 copy-done.1
  137.9 0.9 gather_fusion.5
  138.8 0.7 reduce.4
  139.4 0.9 reshape.198
  140.3 9.2 %all-to-all-start.4 = ((bf16[128,2,512]{2,1,0:T(2,128)(2,1)}), bf16[128,2,512]{2,1,0:T(2,128)(2,1)S(1)}, u32[]{:S(2)}, u32[]{:S(2)}) async-start(bf16[128,2,512]{2,1,0:T(2,128)(2,1)} %reshape.198), calls=%async_computation.6 | async-start | bytes 524288 | tf_op jit(solution)/shard_map/all_to_all | solution.py:51
  149.5 0.9 gather_fusion.7
  150.4 0.7 reduce.3
  151.1 0.9 reshape.200
  152.0 8.7 %all-to-all-done.4 = bf16[128,2,512]{2,1,0:T(2,128)(2,1)S(1)} async-done(((bf16[128,2,512]{2,1,0:T(2,128)(2,1)}), bf16[128,2,512]{2,1,0:T(2,128)(2,1)S(1)}, u32[]{:S(2)}, u32[]{:S(2)}) %all-to-all-start.4) | async-done | bytes 262176 | tf_op jit(solution)/shard_map/all_to_all | solution.py:51
  160.6 4.4 %all-to-all-start.5 = ((bf16[128,2,512]{2,1,0:T(2,128)(2,1)}), bf16[128,2,512]{2,1,0:T(2,128)(2,1)S(1)}, u32[]{:S(2)}, u32[]{:S(2)}) async-start(bf16[128,2,512]{2,1,0:T(2,128)(2,1)} %reshape.200), calls=%async_computation.7 | async-start | bytes 524288 | tf_op jit(solution)/shard_map/all_to_all | solution.py:52
  165.0 1.1 gather_fusion
  166.2 1.2 reduce.2
  167.4 1.1 reshape.196
  168.5 7.6 %all-to-all-done.5 = bf16[128,2,512]{2,1,0:T(2,128)(2,1)S(1)} async-done(((bf16[128,2,512]{2,1,0:T(2,128)(2,1)}), bf16[128,2,512]{2,1,0:T(2,128)(2,1)S(1)}, u32[]{:S(2)}, u32[]{:S(2)}) %all-to-all-start.5) | async-done | bytes 262176 | tf_op jit(solution)/shard_map/all_to_all | solution.py:52
  176.1 5.1 %all-to-all-start.1 = ((bf16[128,2,1792]{2,1,0:T(2,128)(2,1)}), bf16[128,2,1792]{2,1,0:T(2,128)(2,1)}, u32[]{:S(2)}, u32[]{:S(2)}) async-start(bf16[128,2,1792]{2,1,0:T(2,128)(2,1)} %reshape.196), calls=%async_computation.2 | async-start | bytes 1835008 | tf_op jit(solution)/shard_map/all_to_all | solution.py:50
  181.3 0.2 reshape.199
  181.6 0.9 gather_fusion.6
  182.5 0.2 reshape.201
  182.8 0.9 gather_fusion.8
  183.7 0.8 bitcast_bitcast_fusion
  184.5 14.5 %all-to-all-done.1 = bf16[128,2,1792]{2,1,0:T(2,128)(2,1)} async-done(((bf16[128,2,1792]{2,1,0:T(2,128)(2,1)}), bf16[128,2,1792]{2,1,0:T(2,128)(2,1)}, u32[]{:S(2)}, u32[]{:S(2)}) %all-to-all-start.1) | async-done | bytes 917536 | tf_op jit(solution)/shard_map/all_to_all | solution.py:50
  199.0 5.4 %reshape.197 = bf16[128,1,3584]{2,1,0:T(2,128)(2,1)S(1)} reshape(bf16[128,2,1792]{2,1,0:T(2,128)(2,1)} %all-to-all-done.1) | data formatting | bytes 1835008
  204.6 1.1 gather_fusion.2
  205.7 1.4 fusion.15
  207.2 2.5 %fusion.18 = bf16[128,3584]{1,0:T(8,128)(2,1)} fusion(bf16[128,3584]{1,0:T(8,128)(2,1)} %reduce-scatter.5.cloned.1.call-done, bf16[128,3584]{1,0:T(8,128)(2,1)S(1)} %gather_fusion.2, f32[3584]{0:T(1024)S(1)} %copy-done.6, f32[128]{0:T(128)S(1)} %add_rsqrt_fusion), kind=kLoop, calls=%fused_computation.37 | loop fusion | flops 2752512 | bytes 2767360 | tf_op jit(solution)/shard_map/convert_element_type | solution.py:131
  (41 shorter events, 0.6 us)
Async XLA Ops:
  7.2 37.5 %reduce-scatter.3.cloned.1.call-start = ((), (), s32[]{:S(2)}) async-start(), calls=%async_computation.8 | async-start | bytes 2752512 | tf_op jit(solution)/shard_map/reduce_scatter | solution.py:98
  7.9 6.5 %collective-permute-start.1 = (s32[128]{0:T(128)S(1)}, s32[128]{0:T(128)S(1)}, u32[]{:S(2)}, u32[]{:S(2)}) collective-permute-start(s32[128]{0:T(128)S(1)} %broadcast_add_fusion), channel_id=1, source_target_pairs={{0,1},{2,3},{4,5},{6,7},{8,9},{10,11},{12,13},{14,15},{16,17},{18,... | collective-permute-start | bytes 1544 | tf_op jit(solution)/shard_map/ppermute | solution.py:17
  10.3 6.4 %collective-permute-start.2 = (bf16[128,1024]{0,1:T(8,128)(2,1)S(1)}, bf16[128,1024]{0,1:T(8,128)(2,1)S(1)}, u32[]{:S(2)}, u32[]{:S(2)}) collective-permute-start(bf16[128,1024]{0,1:T(8,128)(2,1)S(1)} %copy.46), channel_id=1, source_target_pairs={{0,1},{2,3},{4,5},{6,7},{8,9},{10,11},{12,13},{14,15},{16,17},{18,... | collective-permute-start | bytes 786440 | tf_op jit(solution)/shard_map/ppermute | solution.py:17
  11.6 4.0 %collective-permute-start = (bf16[128,1024]{1,0:T(8,128)(2,1)}, bf16[128,1024]{1,0:T(8,128)(2,1)S(1)}, u32[]{:S(2)}, u32[]{:S(2)}) collective-permute-start(bf16[128,1024]{1,0:T(8,128)(2,1)} %param.15), channel_id=1, source_target_pairs={{0,1},{2,3},{4,5},{6,7},{8,9},{10,11},{12,13},{14,15},{16,17},{18,... | collective-permute-start | bytes 786440 | tf_op jit(solution)/shard_map/ppermute | solution.py:17
  28.6 0.7 copy-start
  28.6 17.6 %copy-start.3 = (bf16[128,3584]{1,0:T(8,128)(2,1)S(1)}, bf16[128,3584]{1,0:T(8,128)(2,1)}, u32[]{:S(2)}) copy-start(bf16[128,3584]{1,0:T(8,128)(2,1)} %param.16) | copy-start | bytes 2752516
  28.6 17.6 %copy-start.4 = (f32[3584]{0:T(1024)S(1)}, f32[3584]{0:T(1024)}, u32[]{:S(2)}) copy-start(f32[3584]{0:T(1024)} %param.20) | copy-start | bytes 43012
  33.8 20.4 %all-to-all-start.2 = ((s32[128,1,1]{2,1,0:T(1,128)}), s32[128,1,1]{2,1,0:T(1,128)S(1)}, u32[]{:S(2)}, u32[]{:S(2)}) async-start(s32[128,1,1]{2,1,0:T(1,128)} %copy.52), calls=%async_computation.3 | async-start | bytes 131072 | tf_op jit(solution)/shard_map/all_to_all | solution.py:49
  44.7 3.3 %copy-start.5 = (f32[3584]{0:T(1024)S(1)}, f32[3584]{0:T(1024)}, u32[]{:S(2)}) copy-start(f32[3584]{0:T(1024)} %param.21) | copy-start | bytes 43012
  54.2 25.8 %all-to-all-start.3 = ((bf16[128,2,1792]{2,1,0:T(2,128)(2,1)}), bf16[128,2,1792]{2,1,0:T(2,128)(2,1)S(1)}, u32[]{:S(2)}, u32[]{:S(2)}) async-start(bf16[128,2,1792]{2,1,0:T(2,128)(2,1)} %reshape.194), calls=%async_computation.4 | async-start | bytes 1835008 | tf_op jit(solution)/shard_map/all_to_all | solution.py:48
  62.0 33.3 %all-gather.3.cloned.1.call-start = ((), (), s32[]{:S(2)}) async-start(), calls=%async_computation.10 | async-start | bytes 2752512 | tf_op jit(solution)/shard_map/all_gather | solution.py:117
  85.7 120.0 %reduce-scatter.5.cloned.1.call-start = ((), (), s32[]{:S(2)}) async-start(), calls=%async_computation.9 | async-start | bytes 2752512 | tf_op jit(solution)/shard_map/reduce_scatter | solution.py:125
  95.3 17.1 %copy-start.7 = (bf16[256,3584]{1,0:T(8,128)(2,1)S(1)}, bf16[256,3584]{1,0:T(8,128)(2,1)}, u32[]{:S(2)}) copy-start(bf16[256,3584]{1,0:T(8,128)(2,1)} %all-gather.3.cloned.1.call-done) | copy-start | bytes 5505028
  136.9 0.9 copy-start.1
  137.9 11.6 %copy-start.2 = (bf16[128,1024]{1,0:T(8,128)(2,1)S(1)}, bf16[128,1024]{1,0:T(8,128)(2,1)}, u32[]{:S(2)}) copy-start(bf16[128,1024]{1,0:T(8,128)(2,1)} %param.15) | copy-start | bytes 786436
  140.3 20.3 %all-to-all-start.4 = ((bf16[128,2,512]{2,1,0:T(2,128)(2,1)}), bf16[128,2,512]{2,1,0:T(2,128)(2,1)S(1)}, u32[]{:S(2)}, u32[]{:S(2)}) async-start(bf16[128,2,512]{2,1,0:T(2,128)(2,1)} %reshape.198), calls=%async_computation.6 | async-start | bytes 524288 | tf_op jit(solution)/shard_map/all_to_all | solution.py:51
  160.6 15.5 %all-to-all-start.5 = ((bf16[128,2,512]{2,1,0:T(2,128)(2,1)}), bf16[128,2,512]{2,1,0:T(2,128)(2,1)S(1)}, u32[]{:S(2)}, u32[]{:S(2)}) async-start(bf16[128,2,512]{2,1,0:T(2,128)(2,1)} %reshape.200), calls=%async_computation.7 | async-start | bytes 524288 | tf_op jit(solution)/shard_map/all_to_all | solution.py:52
  176.1 22.9 %all-to-all-start.1 = ((bf16[128,2,1792]{2,1,0:T(2,128)(2,1)}), bf16[128,2,1792]{2,1,0:T(2,128)(2,1)}, u32[]{:S(2)}, u32[]{:S(2)}) async-start(bf16[128,2,1792]{2,1,0:T(2,128)(2,1)} %reshape.196), calls=%async_computation.2 | async-start | bytes 1835008 | tf_op jit(solution)/shard_map/all_to_all | solution.py:50
  204.6 2.6 %copy-start.6 = (f32[3584]{0:T(1024)S(1)}, f32[3584]{0:T(1024)}, u32[]{:S(2)}) copy-start(f32[3584]{0:T(1024)} %param.25) | copy-start | bytes 43012
Sparse Core Ops, SparseCore 0:
  28.7 15.0 reduce-scatter.2
  85.9 9.4 all-gather.2
  137.1 13.3 reduce-scatter.4
where the time goes:
time: 217 us; the launch traced here: 216 us
  waiting for transfers between devices  56.2 us (26%)
  matrix products  48.9 us (23%)
  starting transfers between devices  41.6 us (19%)
  local copies, waits for them, and re-layouts  30.5 us (14%)
  other arithmetic  20.6 us (9%)
  between operations  14.1 us (6%)
  blocking collectives  4.22 us (2%)
    dot_general x1, matrix products, per_device(): jnp.dot(active, down_weight, preferred_element_type=jnp.float32)  24.6 us
    dot_general x1, matrix products, per_device(): gate_part = jnp.dot(picked, gate_weight, preferred_element_type=jnp.float32)  17.1 us
    unnamed x29, local copies, waits for them, and re-layouts  16.6 us
    all_to_all x1, waiting for transfers between devices, send_rows(): lax.all_to_all(stream_part, ('req', 'kv'), split_axis=0, concat_axis=0, t...  14.5 us
    all_to_all x1, waiting for transfers between devices, send_rows(): lax.all_to_all(normed_part, ('req', 'kv'), split_axis=0, concat_axis=0, t...  13 us
    all_to_all x1, starting transfers between devices, send_rows(): lax.all_to_all(normed_pos, ('req', 'kv'), split_axis=0, concat_axis=0, ti...  10.9 us
    all_gather x1, waiting for transfers between devices, per_device(): group_normed = lax.all_gather(own_normed, 'kv', axis=0, tiled=True)  9.35 us
    all_to_all x1, starting transfers between devices, send_rows(): lax.all_to_all(key_portion, ('req', 'kv'), split_axis=0, concat_axis=0, t...  9.19 us
  transfers between devices with their start and end apart: 11, of which 7 were waited for; matrix products, arithmetic and copies ran while one was open for 18% of the time, Pallas kernels for 0%

commit v1 on v0

--- a/solution.py
+++ b/solution.py
@@ -114,7 +114,9 @@
     )
     placed = jnp.argsort(received[1])
     own_normed = received[0][placed]
-    group_normed = lax.all_gather(own_normed, "kv", axis=0, tiled=True)
+    group_normed = jnp.concatenate(
+        lax.all_to_all(jnp.stack([own_normed] * lax.axis_size("kv")), "kv", 0, 0), axis=0
+    )
     own_stream = received[2][placed]
     resident_keys = received[3][placed]
     resident_values = received[4][placed]

time: 217 us -> 204 us (0.940)
  waiting for transfers between devices: 56.2 us -> 46.9 us
  blocking collectives: 4.22 us -> 9.99 us
  starting transfers between devices: 41.6 us -> 36 us
  matrix products: 48.9 us -> 45.5 us
    all_gather x1 -> x0, waiting for transfers between devices: 9.35 us -> none  [per_device(): group_normed = lax.all_gather(own_normed, 'kv', axis=0, tiled=True)]
    all_to_all x0 -> x1, blocking collectives: none -> 5.77 us  [per_device(): lax.all_to_all(jnp.stack([own_normed] * lax.axis_size('kv')), 'kv', 0, 0)]
    all_to_all x1, starting transfers between devices: 9.19 us -> 3.82 us  [send_rows(): lax.all_to_all(key_portion, ('req', 'kv'), split_axis=0, concat_axis=0, t...]
    dot_general x1, matrix products: 17.1 us -> 13.7 us  [per_device(): gate_part = jnp.dot(picked, gate_weight, preferred_element_type=jnp.float32)]
    unnamed x29 -> x27, local copies, waits for them, and re-layouts: 16.6 us -> 16.6 us
  transfers between devices with their start and end apart: 11 -> 10, of which waited for: 7 -> 6; matrix products, arithmetic and copies ran while one was open for 18% -> 19% of each run, Pallas kernels for 0% -> 0%
where the time goes in v1:
time: 204 us; the launch traced here: 203 us
  waiting for transfers between devices  46.9 us (23%)
  matrix products  45.5 us (22%)
  starting transfers between devices  36 us (18%)
  local copies, waits for them, and re-layouts  29.6 us (15%)
  other arithmetic  20.8 us (10%)
  between operations  14.4 us (7%)
  blocking collectives  9.99 us (5%)
    dot_general x1, matrix products, per_device(): jnp.dot(active, down_weight, preferred_element_type=jnp.float32)  24.6 us
    unnamed x27, local copies, waits for them, and re-layouts  16.6 us
    all_to_all x1, waiting for transfers between devices, send_rows(): lax.all_to_all(stream_part, ('req', 'kv'), split_axis=0, concat_axis=0, t...  14.5 us
    dot_general x1, matrix products, per_device(): gate_part = jnp.dot(picked, gate_weight, preferred_element_type=jnp.float32)  13.7 us
    all_to_all x1, waiting for transfers between devices, send_rows(): lax.all_to_all(normed_part, ('req', 'kv'), split_axis=0, concat_axis=0, t...  13 us
    all_to_all x1, starting transfers between devices, send_rows(): lax.all_to_all(normed_pos, ('req', 'kv'), split_axis=0, concat_axis=0, ti...  10.9 us
    all_to_all x1, waiting for transfers between devices, send_rows(): lax.all_to_all(key_portion, ('req', 'kv'), split_axis=0, concat_axis=0, t...  8.71 us
    all_to_all x1, starting transfers between devices, send_rows(): lax.all_to_all(normed_part, ('req', 'kv'), split_axis=0, concat_axis=0, t...  7.8 us
  transfers between devices with their start and end apart: 10, of which 6 were waited for; matrix products, arithmetic and copies ran while one was open for 19% of the time, Pallas kernels for 0%

profile of v1, /device:TPU:1, one launch (start us, length us, event | category | flops | bytes accessed | tf_op | source)
XLA Modules:
  0.0 203.2 jit_solution(318032628038433108)
XLA Ops:
  7.2 0.7 broadcast_add_fusion
  7.9 1.3 collective-permute-start.1
  9.2 1.1 copy.46
  10.3 1.3 collective-permute-start.2
  11.6 1.3 collective-permute-start
  12.9 1.4 reshape.109
  14.4 0.1 fusion.35
  14.5 1.0 collective-permute-done
  15.5 1.0 pad_maximum_fusion.1
  16.5 0.2 copy.44
  16.8 0.6 fusion.42
  17.4 0.3 fusion.29
  17.7 0.2 copy.50
  17.9 4.2 %all_to_all.81 = bf16[128,2,1024]{2,0,1:T(8,128)(2,1)S(1)} all-to-all(bf16[128,2,1024]{2,0,1:T(8,128)(2,1)S(1)} %copy.50), channel_id=1, replica_groups=mesh['req'=64,'kv'=2] {'kv'}, dimensions={1} | all-to-all | bytes 1048576 | tf_op jit(solution)/shard_map/all_to_all | solution.py:96
  22.1 6.4 %convolution_convert_fusion.1 = bf16[256,3584]{1,0:T(8,128)(2,1)} fusion(bf16[256,1024]{1,0:T(8,128)(2,1)S(1)} %bitcast.81, bf16[1024,3584]{1,0:T(8,128)(2,1)} %param.19), kind=kOutput, calls=%fused_computation.13 | convolution fusion | flops 1879965696 | bytes 9699328 | tf_op jit(solution)/shard_map/dot_general | solution.py:99
  28.6 0.6 copy-done
  29.2 2.5 %sort.31 = (s32[128]{0:T(128)}, s32[128]{0:T(128)S(1)}) sort(s32[128]{0:T(128)S(1)} %copy-done, s32[128]{0:T(128)S(1)} %iota.18), dimensions={0}, to_apply=%region_3.4 | sort | flops 896 | bytes 2048 | tf_op jit(solution)/shard_map/jit(argsort)/sort | solution.py:106
  31.8 1.2 gather_fusion.1
  33.0 0.7 copy.52
  33.8 10.9 %all-to-all-start.2 = ((s32[128,1,1]{2,1,0:T(1,128)}), s32[128,1,1]{2,1,0:T(1,128)S(1)}, u32[]{:S(2)}, u32[]{:S(2)}) async-start(s32[128,1,1]{2,1,0:T(1,128)} %copy.52), calls=%async_computation.3 | async-start | bytes 131072 | tf_op jit(solution)/shard_map/all_to_all | solution.py:49
  44.7 1.4 fusion.8
  46.2 1.8 fusion.12
  48.0 0.3 fusion.14
  48.3 1.1 gather_fusion.3
  49.4 0.5 broadcast.147
  49.9 1.2 reduce.1
  51.1 1.1 reshape.197
  52.2 2.0 all-to-all-done.2
  54.2 7.8 %all-to-all-start.3 = ((bf16[128,2,1792]{2,1,0:T(2,128)(2,1)}), bf16[128,2,1792]{2,1,0:T(2,128)(2,1)S(1)}, u32[]{:S(2)}, u32[]{:S(2)}) async-start(bf16[128,2,1792]{2,1,0:T(2,128)(2,1)} %reshape.197), calls=%async_computation.4 | async-start | bytes 1835008 | tf_op jit(solution)/shard_map/all_to_all | solution.py:48
  62.0 2.4 %reduce = s32[128]{0:T(128)S(1)} reduce(s32[128,1,1]{2,1,0:T(1,128)S(1)} %all-to-all-done.2, s32[]{:T(128)} %constant.17.clone.1), dimensions={1,2}, to_apply=%all_to_all.62.reduce_sub_computation | reduce | bytes 1028 | tf_op jit(solution)/shard_map/all_to_all | solution.py:49
  64.4 2.5 %sort.32 = (s32[128]{0:T(128)}, s32[128]{0:T(128)S(1)}) sort(s32[128]{0:T(128)S(1)} %reduce, s32[128]{0:T(128)S(1)} %iota.19), dimensions={0}, to_apply=%region_4.5 | sort | flops 896 | bytes 2048 | tf_op jit(solution)/shard_map/jit(argsort)/sort | solution.py:115
  67.0 13.0 %all-to-all-done.3 = bf16[128,2,1792]{2,1,0:T(2,128)(2,1)S(1)} async-done(((bf16[128,2,1792]{2,1,0:T(2,128)(2,1)}), bf16[128,2,1792]{2,1,0:T(2,128)(2,1)S(1)}, u32[]{:S(2)}, u32[]{:S(2)}) %all-to-all-start.3) | async-done | bytes 917536 | tf_op jit(solution)/shard_map/all_to_all | solution.py:48
  79.9 2.1 %reshape.198 = bf16[128,1,3584]{2,1,0:T(2,128)(2,1)} reshape(bf16[128,2,1792]{2,1,0:T(2,128)(2,1)S(1)} %all-to-all-done.3) | data formatting | bytes 1835008
  82.0 1.6 copy.79
  83.7 1.1 gather_fusion.4
  84.8 0.2 pad_maximum_fusion
  85.0 5.8 %all_to_all.82 = bf16[2,128,3584]{2,1,0:T(8,128)(2,1)S(1)} all-to-all(bf16[2,128,3584]{2,1,0:T(8,128)(2,1)S(1)} %pad_maximum_fusion), channel_id=1, replica_groups=mesh['req'=64,'kv'=2] {'kv'}, dimensions={0} | all-to-all | bytes 3670016 | tf_op jit(solution)/shard_map/all_to_all | solution.py:118
  90.7 13.7 %fusion.43 = f32[256,3584]{1,0:T(8,128)} fusion(bf16[256,3584]{1,0:T(8,128)(2,1)S(1)} %bitcast.72, bf16[3584,3584]{1,0:T(8,128)(2,1)} %param.22), kind=kOutput, calls=%fused_computation.87 | convolution fusion | flops 6576668672 | bytes 31195136 | tf_op jit(solution)/shard_map/dot_general | solution.py:124
  104.4 24.6 %convolution_convert_fusion = bf16[256,3584]{1,0:T(8,128)(2,1)} fusion(bf16[3584,3584]{1,0:T(8,128)(2,1)} %param.24, bf16[256,3584]{1,0:T(8,128)(2,1)S(1)} %bitcast.73, bf16[3584,3584]{1,0:T(8,128)(2,1)} %param.23, f32[256,3584]{1,0:T(8,128)} %fusion.43), kind=kOutput, calls=%fused_computation.12 | convolution fusion | flops 13163429888 | bytes 58720256 | tf_op jit(solution)/shard_map/dot_general | solution.py:128
  129.0 0.9 copy-done.1
  129.9 0.9 gather_fusion.5
  130.8 0.7 reduce.4
  131.5 0.9 reshape.201
  132.3 3.8 %all-to-all-start.5 = ((bf16[128,2,512]{2,1,0:T(2,128)(2,1)}), bf16[128,2,512]{2,1,0:T(2,128)(2,1)S(1)}, u32[]{:S(2)}, u32[]{:S(2)}) async-start(bf16[128,2,512]{2,1,0:T(2,128)(2,1)} %reshape.201), calls=%async_computation.7 | async-start | bytes 524288 | tf_op jit(solution)/shard_map/all_to_all | solution.py:51
  136.2 0.9 gather_fusion.7
  137.0 0.7 reduce.3
  137.7 0.9 reshape.203
  138.6 8.7 %all-to-all-done.5 = bf16[128,2,512]{2,1,0:T(2,128)(2,1)S(1)} async-done(((bf16[128,2,512]{2,1,0:T(2,128)(2,1)}), bf16[128,2,512]{2,1,0:T(2,128)(2,1)S(1)}, u32[]{:S(2)}, u32[]{:S(2)}) %all-to-all-start.5) | async-done | bytes 262176 | tf_op jit(solution)/shard_map/all_to_all | solution.py:51
  147.3 4.4 %all-to-all-start.6 = ((bf16[128,2,512]{2,1,0:T(2,128)(2,1)}), bf16[128,2,512]{2,1,0:T(2,128)(2,1)S(1)}, u32[]{:S(2)}, u32[]{:S(2)}) async-start(bf16[128,2,512]{2,1,0:T(2,128)(2,1)} %reshape.203), calls=%async_computation.8 | async-start | bytes 524288 | tf_op jit(solution)/shard_map/all_to_all | solution.py:52
  151.7 1.1 gather_fusion
  152.9 1.2 reduce.2
  154.1 1.1 reshape.199
  155.2 7.6 %all-to-all-done.6 = bf16[128,2,512]{2,1,0:T(2,128)(2,1)S(1)} async-done(((bf16[128,2,512]{2,1,0:T(2,128)(2,1)}), bf16[128,2,512]{2,1,0:T(2,128)(2,1)S(1)}, u32[]{:S(2)}, u32[]{:S(2)}) %all-to-all-start.6) | async-done | bytes 262176 | tf_op jit(solution)/shard_map/all_to_all | solution.py:52
  162.8 5.1 %all-to-all-start.1 = ((bf16[128,2,1792]{2,1,0:T(2,128)(2,1)}), bf16[128,2,1792]{2,1,0:T(2,128)(2,1)}, u32[]{:S(2)}, u32[]{:S(2)}) async-start(bf16[128,2,1792]{2,1,0:T(2,128)(2,1)} %reshape.199), calls=%async_computation.2 | async-start | bytes 1835008 | tf_op jit(solution)/shard_map/all_to_all | solution.py:50
  168.0 0.2 reshape.202
  168.3 0.9 gather_fusion.6
  169.2 0.2 reshape.204
  169.5 0.9 gather_fusion.8
  170.4 0.8 bitcast_bitcast_fusion
  171.2 14.5 %all-to-all-done.1 = bf16[128,2,1792]{2,1,0:T(2,128)(2,1)} async-done(((bf16[128,2,1792]{2,1,0:T(2,128)(2,1)}), bf16[128,2,1792]{2,1,0:T(2,128)(2,1)}, u32[]{:S(2)}, u32[]{:S(2)}) %all-to-all-start.1) | async-done | bytes 917536 | tf_op jit(solution)/shard_map/all_to_all | solution.py:50
  185.7 5.4 %reshape.200 = bf16[128,1,3584]{2,1,0:T(2,128)(2,1)S(1)} reshape(bf16[128,2,1792]{2,1,0:T(2,128)(2,1)} %all-to-all-done.1) | data formatting | bytes 1835008
  191.3 1.1 gather_fusion.2
  192.4 1.4 fusion.15
  193.9 2.5 %fusion.18 = bf16[128,3584]{1,0:T(8,128)(2,1)} fusion(bf16[128,3584]{1,0:T(8,128)(2,1)} %reduce-scatter.5.cloned.1.call-done, bf16[128,3584]{1,0:T(8,128)(2,1)S(1)} %gather_fusion.2, f32[3584]{0:T(1024)S(1)} %copy-done.6, f32[128]{0:T(128)S(1)} %add_rsqrt_fusion), kind=kLoop, calls=%fused_computation.37 | loop fusion | flops 2752512 | bytes 2767360 | tf_op jit(solution)/shard_map/convert_element_type | solution.py:133
  (38 shorter events, 0.6 us)
Async XLA Ops:
  7.2 37.5 %reduce-scatter.3.cloned.1.call-start = ((), (), s32[]{:S(2)}) async-start(), calls=%async_computation.9 | async-start | bytes 2752512 | tf_op jit(solution)/shard_map/reduce_scatter | solution.py:98
  7.9 6.5 %collective-permute-start.1 = (s32[128]{0:T(128)S(1)}, s32[128]{0:T(128)S(1)}, u32[]{:S(2)}, u32[]{:S(2)}) collective-permute-start(s32[128]{0:T(128)S(1)} %broadcast_add_fusion), channel_id=1, source_target_pairs={{0,1},{2,3},{4,5},{6,7},{8,9},{10,11},{12,13},{14,15},{16,17},{18,... | collective-permute-start | bytes 1544 | tf_op jit(solution)/shard_map/ppermute | solution.py:17
  10.3 6.4 %collective-permute-start.2 = (bf16[128,1024]{0,1:T(8,128)(2,1)S(1)}, bf16[128,1024]{0,1:T(8,128)(2,1)S(1)}, u32[]{:S(2)}, u32[]{:S(2)}) collective-permute-start(bf16[128,1024]{0,1:T(8,128)(2,1)S(1)} %copy.46), channel_id=1, source_target_pairs={{0,1},{2,3},{4,5},{6,7},{8,9},{10,11},{12,13},{14,15},{16,17},{18,... | collective-permute-start | bytes 786440 | tf_op jit(solution)/shard_map/ppermute | solution.py:17
  11.6 4.0 %collective-permute-start = (bf16[128,1024]{1,0:T(8,128)(2,1)}, bf16[128,1024]{1,0:T(8,128)(2,1)S(1)}, u32[]{:S(2)}, u32[]{:S(2)}) collective-permute-start(bf16[128,1024]{1,0:T(8,128)(2,1)} %param.15), channel_id=1, source_target_pairs={{0,1},{2,3},{4,5},{6,7},{8,9},{10,11},{12,13},{14,15},{16,17},{18,... | collective-permute-start | bytes 786440 | tf_op jit(solution)/shard_map/ppermute | solution.py:17
  28.6 0.7 copy-start
  28.6 17.6 %copy-start.3 = (bf16[128,3584]{1,0:T(8,128)(2,1)S(1)}, bf16[128,3584]{1,0:T(8,128)(2,1)}, u32[]{:S(2)}) copy-start(bf16[128,3584]{1,0:T(8,128)(2,1)} %param.16) | copy-start | bytes 2752516
  28.6 17.6 %copy-start.4 = (f32[3584]{0:T(1024)S(1)}, f32[3584]{0:T(1024)}, u32[]{:S(2)}) copy-start(f32[3584]{0:T(1024)} %param.20) | copy-start | bytes 43012
  33.8 20.4 %all-to-all-start.2 = ((s32[128,1,1]{2,1,0:T(1,128)}), s32[128,1,1]{2,1,0:T(1,128)S(1)}, u32[]{:S(2)}, u32[]{:S(2)}) async-start(s32[128,1,1]{2,1,0:T(1,128)} %copy.52), calls=%async_computation.3 | async-start | bytes 131072 | tf_op jit(solution)/shard_map/all_to_all | solution.py:49
  44.7 3.3 %copy-start.5 = (f32[3584]{0:T(1024)S(1)}, f32[3584]{0:T(1024)}, u32[]{:S(2)}) copy-start(f32[3584]{0:T(1024)} %param.21) | copy-start | bytes 43012
  54.2 25.8 %all-to-all-start.3 = ((bf16[128,2,1792]{2,1,0:T(2,128)(2,1)}), bf16[128,2,1792]{2,1,0:T(2,128)(2,1)S(1)}, u32[]{:S(2)}, u32[]{:S(2)}) async-start(bf16[128,2,1792]{2,1,0:T(2,128)(2,1)} %reshape.197), calls=%async_computation.4 | async-start | bytes 1835008 | tf_op jit(solution)/shard_map/all_to_all | solution.py:48
  62.0 130.4 %reduce-scatter.5.cloned.1.call-start = ((), (), s32[]{:S(2)}) async-start(), calls=%async_computation.10 | async-start | bytes 2752512 | tf_op jit(solution)/shard_map/reduce_scatter | solution.py:127
  129.0 0.9 copy-start.1
  129.9 6.3 %copy-start.2 = (bf16[128,1024]{1,0:T(8,128)(2,1)S(1)}, bf16[128,1024]{1,0:T(8,128)(2,1)}, u32[]{:S(2)}) copy-start(bf16[128,1024]{1,0:T(8,128)(2,1)} %param.15) | copy-start | bytes 786436
  132.3 15.0 %all-to-all-start.5 = ((bf16[128,2,512]{2,1,0:T(2,128)(2,1)}), bf16[128,2,512]{2,1,0:T(2,128)(2,1)S(1)}, u32[]{:S(2)}, u32[]{:S(2)}) async-start(bf16[128,2,512]{2,1,0:T(2,128)(2,1)} %reshape.201), calls=%async_computation.7 | async-start | bytes 524288 | tf_op jit(solution)/shard_map/all_to_all | solution.py:51
  147.3 15.5 %all-to-all-start.6 = ((bf16[128,2,512]{2,1,0:T(2,128)(2,1)}), bf16[128,2,512]{2,1,0:T(2,128)(2,1)S(1)}, u32[]{:S(2)}, u32[]{:S(2)}) async-start(bf16[128,2,512]{2,1,0:T(2,128)(2,1)} %reshape.203), calls=%async_computation.8 | async-start | bytes 524288 | tf_op jit(solution)/shard_map/all_to_all | solution.py:52
  162.8 22.9 %all-to-all-start.1 = ((bf16[128,2,1792]{2,1,0:T(2,128)(2,1)}), bf16[128,2,1792]{2,1,0:T(2,128)(2,1)}, u32[]{:S(2)}, u32[]{:S(2)}) async-start(bf16[128,2,1792]{2,1,0:T(2,128)(2,1)} %reshape.199), calls=%async_computation.2 | async-start | bytes 1835008 | tf_op jit(solution)/shard_map/all_to_all | solution.py:50
  191.3 2.6 %copy-start.6 = (f32[3584]{0:T(1024)S(1)}, f32[3584]{0:T(1024)}, u32[]{:S(2)}) copy-start(f32[3584]{0:T(1024)} %param.25) | copy-start | bytes 43012
Sparse Core Ops, SparseCore 0:
  28.7 15.0 reduce-scatter.2
  129.1 7.9 reduce-scatter.4
